TPU v7x, 512 devices: a whole 4x4x16 slice. The times are simulated.
512 devices in a mesh: wa: 4 (over x), vert: 128 (over y, z, core).
Axes of the slice: x: 4, y: 4, z: 16, core: 2. Of those that a mesh axis runs over, the one named last changes fastest.
Arguments:
- hidden: bfloat16 [16384, 1024], P('vert', 'wa'), as said below
- norm_gain: bfloat16 [1024], P('wa'), may hold values from 0.5 to 1.5
- head_weight: bfloat16 [1024, 32128], P('wa', 'vert'), as said below
- target_ids: int32 [16384], P('vert'), may hold values from 0 to 32127
- seq_lengths: int32 [65], replicated, may hold values from 1 to 8192, as said below
Outputs:
- token_logprob: float32 [16384], P('vert')
- token_entropy: float32 [16384], P('vert')
Inputs may be any that keep to these rules, and one draw needn't show every extreme that they name: `seq_lengths`: entry 0 equals 8192; every other entry lies between 1 and 128, and at least one of them equals 128. `hidden`: hidden states of any scale per slot; the norm removes it. `head_weight`: entries of order 3 / sqrt(1024) times a per-column scale.
All inputs are finite; a program needn't handle non-finite values.
Results may differ from a plain program's by a relative error of at most 0.012.
The roundings to bfloat16 on the way count: a program that leaves them out, or rounds other values in their place, can miss the bound.
Values may be sent and summed in bfloat16 or wider, within the bound.
A program may use at most 64 MiB of HBM per device.

v0:
```python
import jax
import jax.numpy as jnp
from jax import lax
from jax.sharding import Mesh
from jax.sharding import PartitionSpec as P

D = 1024
SHORT = 128
norm_epsilon = 1e-06
VERT = ("y", "z", "c")
TOKEN_AXES = ("z", "c")


def live_mask(positions, seq_lengths, long_len, short_len):
    is_long = positions < long_len
    beyond = jnp.maximum(positions - long_len, 0)
    seq_index = jnp.where(is_long, 0, 1 + beyond // short_len)
    offset = jnp.where(is_long, positions, beyond % short_len)
    return offset < jnp.take(seq_lengths, seq_index)


def per_device(hidden, norm_gain, head_weight, target_ids, seq_lengths):
    x_count = lax.axis_size("x")
    y_count = lax.axis_size("y")
    z_count = lax.axis_size("z")
    c_count = lax.axis_size("c")
    x_index = lax.axis_index("x")
    y_index = lax.axis_index("y")
    z_index = lax.axis_index("z")
    c_index = lax.axis_index("c")
    vert_count = y_count * z_count * c_count
    vert_index = (y_index * z_count + z_index) * c_count + c_index
    tok_local = hidden.shape[0]
    quarter = tok_local // x_count
    vocab_local = head_weight.shape[1]
    group_count = z_count * c_count
    rows = lax.all_to_all(hidden, "x", split_axis=0, concat_axis=1, tiled=True)
    gain_full = lax.all_gather(norm_gain, "x", axis=0, tiled=True)
    values = rows.astype(jnp.float32)
    squares = jnp.sum(values * values, axis=1, keepdims=True)
    normed = (
        values * lax.rsqrt(squares / D + norm_epsilon) * gain_full.astype(jnp.float32)
    ).astype(jnp.bfloat16)
    group_rows = lax.all_gather(normed, TOKEN_AXES, axis=0, tiled=True)
    group_ids = lax.all_gather(target_ids, TOKEN_AXES, axis=0)
    group_ids = lax.dynamic_slice_in_dim(group_ids, x_index * quarter, quarter, 1).reshape(-1)
    weight = lax.all_gather(head_weight, ("x", "y"), axis=0)
    weight = weight.reshape(x_count, y_count, D // x_count, vocab_local)
    logits = jnp.einsum(
        "txd,xyde->tye",
        group_rows.reshape(-1, x_count, D // x_count),
        weight,
        preferred_element_type=jnp.float32,
    )
    block_of = (
        lax.broadcasted_iota(jnp.int32, (1, y_count, vocab_local), 1) * z_count + z_index
    ) * c_count + c_index
    column_ids = block_of * vocab_local + lax.broadcasted_iota(
        jnp.int32, (1, y_count, vocab_local), 2
    )
    row_peak = jnp.max(logits, axis=(1, 2))
    scaled = jnp.exp(logits - row_peak[:, None, None])
    row_sum = jnp.sum(scaled, axis=(1, 2))
    row_weighted = jnp.sum(scaled * logits, axis=(1, 2))
    row_picked = jnp.sum(
        jnp.where(column_ids == group_ids[:, None, None], logits, 0.0), axis=(1, 2)
    )
    stats = jnp.stack([row_peak, row_sum, row_weighted, row_picked]).reshape(
        4, group_count, quarter
    )
    parts = lax.all_to_all(stats, TOKEN_AXES, split_axis=1, concat_axis=1, tiled=True)
    part_peak, part_sum, part_weighted, part_picked = (parts[0], parts[1], parts[2], parts[3])
    highest = jnp.max(part_peak, axis=0)
    factor = jnp.exp(part_peak - highest[None, :])
    totals = jnp.sum(part_sum * factor, axis=0)
    weighted = jnp.sum(part_weighted * factor, axis=0)
    picked = jnp.sum(part_picked, axis=0)
    log_norm = highest + jnp.log(totals)
    logprob = picked - log_norm
    entropy = log_norm - weighted / totals
    full_logprob, full_entropy = (
        lax.all_gather(logprob, "x", axis=0, tiled=True),
        lax.all_gather(entropy, "x", axis=0, tiled=True),
    )
    positions = vert_index * tok_local + jnp.arange(tok_local, dtype=jnp.int32)
    live_rows = live_mask(positions, seq_lengths, vert_count * tok_local // 2, SHORT)
    return (jnp.where(live_rows, full_logprob, 0.0), jnp.where(live_rows, full_entropy, 0.0))


def solution(mesh):
    wa_count, vert_count = mesh.devices.shape
    y_count = 4
    c_count = 2
    z_count = vert_count // (y_count * c_count)
    fine = Mesh(mesh.devices.reshape(wa_count, y_count, z_count, c_count), ("x",) + VERT)
    in_specs = (P(VERT, "x"), P("x"), P("x", VERT), P(VERT), P())
    out_specs = (P(VERT), P(VERT))
    return jax.shard_map(
        per_device, mesh=fine, in_specs=in_specs, out_specs=out_specs, check_vma=False
    )
```

profile of v0, /device:TPU:32, one launch (start us, length us, event | category | flops | bytes accessed | tf_op | source)
XLA Modules:
  0.0 210.9 jit_solution(2471399766707559232)
XLA Ops:
  7.2 0.0 copy-start
  7.2 4.3 %all-to-all-start = ((bf16[4,32,256]{2,1,0:T(8,128)(2,1)}), bf16[4,32,256]{2,1,0:T(8,128)(2,1)S(1)}, u32[]{:S(2)}, u32[]{:S(2)}) async-start(bf16[4,32,256]{2,1,0:T(8,128)(2,1)} %bitcast.53), calls=%async_computation | async-start | bytes 131072 | tf_op jit(solution)/shard_map/all_to_all | solution.py:37
  11.5 0.0 all-gather.7.cloned.1.call-start
  11.5 0.7 reshape.134
  12.1 10.2 %all-gather.2 = bf16[4,1,256]{2,1,0:T(2,128)(2,1)S(1)} all-gather(bf16[1,1,256]{2,1,0:T(2,128)(2,1)S(1)} %reshape.134), channel_id=1, replica_groups=mesh['x'=4,'y'=4,'z'=16,'c'=2] {'x'}, dimensions={0}, use_global_device_ids=true | all-gather | bytes 2560 | tf_op jit(solution)/shard_map/all_gather | solution.py:38
  22.3 0.0 all-to-all-done
  22.4 0.1 fusion.4
  22.5 0.7 multiply_convert_fusion
  23.2 0.0 all-gather.7.cloned.1.call-update
  23.2 0.0 all-gather.9.cloned.1.call-start
  23.3 0.7 all-gather.9.cloned.1.call-update
  24.0 34.1 %all-gather.3 = s32[32,1,128]{2,1,0:T(1,128)S(1)} all-gather(s32[1,1,128]{2,1,0:T(1,128)} %bitcast.55), channel_id=3, replica_groups=mesh['x'=4,'y'=4,'z'=16,'c'=2] {'z','c'}, dimensions={0}, use_global_device_ids=true | all-gather | bytes 16896 | tf_op jit(solution)/shard_map/all_gather | solution.py:45
  58.1 0.1 dynamic-slice_reduce_fusion
  58.2 0.1 eq.18
  58.3 1.3 dynamic-slice
  60.2 0.1 iota_add_fusion
  60.3 36.7 %all-gather.7.cloned.1.call-done = bf16[1024,1024]{1,0:T(8,128)(2,1)} async-done(((bf16[32,1024]{1,0:T(8,128)(2,1)}), bf16[1024,1024]{1,0:T(8,128)(2,1)}) %all-gather.7.cloned.1.call-update) | async-done | bytes 2097168 | tf_op jit(solution)/shard_map/all_gather | solution.py:44
  97.0 2.9 %copy.12 = bf16[1024,1024]{0,1:T(8,128)(2,1)S(1)} copy(bf16[1024,1024]{1,0:T(8,128)(2,1)} %all-gather.7.cloned.1.call-done) | data formatting | bytes 4194304 | tf_op jit(solution)/shard_map/all_gather | solution.py:44
  99.9 57.4 %all-gather.9.cloned.1.call-done = bf16[4096,251]{1,0:T(8,128)(2,1)} async-done(((bf16[256,251]{1,0:T(8,128)(2,1)}), bf16[4096,251]{1,0:T(8,128)(2,1)}) %all-gather.9.cloned.1.call-update) | async-done | bytes 2056208 | tf_op jit(solution)/shard_map/all_gather | solution.py:47
  157.3 5.9 %bitcast_reduce_fusion = (f32[1024]{0:T(1024)S(1)}, f32[1024,4,251,1]{0,2,1,3:T(8,128)}) fusion(bf16[1024,4,256,1]{0,2,3,1:T(8,128)(2,1)S(1)} %bitcast.46, bf16[4,4,256,251]{3,2,1,0:T(8,128)(2,1)} %bitcast.56), kind=kOutput, calls=%fused_computation.4 | convolution fusion | flops 2106567680 | bytes 8269824 | tf_op jit(solution)/shard_map/txd,xyde->tye/dot_general | solution.py:49
  163.2 0.1 stack.15
  163.3 2.9 %fusion.1 = (f32[1024]{0:T(1024)S(1)}, f32[1024]{0:T(1024)S(1)}, f32[1024]{0:T(1024)S(1)}) fusion(f32[1024,4,251,1]{0,2,1,3:T(8,128)} %get-tuple-element.16, f32[1024]{0:T(1024)S(1)} %get-tuple-element.15, s32[1024]{0:T(1024)S(1)} %eq.18, s32[4,251]{1,0:T(4,128)S(1)} %iota_add_fusion), kind=kLoop, calls=%fused_computation.6 | loop fusion | flops 7193600 | bytes 4136880 | tf_op jit(solution)/shard_map/reduce_sum | solution.py:63
  166.2 0.1 stack.18
  166.3 0.1 stack.17
  166.4 0.1 stack.16
  166.5 0.1 fusion.9
  166.6 0.7 reshape.155
  167.3 12.8 %all-to-all-start.1 = ((f32[32,1,128]{2,1,0:T(1,128)}), f32[32,1,128]{2,1,0:T(1,128)S(1)}, u32[]{:S(2)}, u32[]{:S(2)}) async-start(f32[32,1,128]{2,1,0:T(1,128)} %reshape.155), calls=%async_computation.1 | async-start | bytes 32768 | tf_op jit(solution)/shard_map/all_to_all | solution.py:71
  180.1 0.0 copy-done
  180.1 1.2 gather_fusion
  181.4 9.9 %all-to-all-done.1 = f32[32,1,128]{2,1,0:T(1,128)S(1)} async-done(((f32[32,1,128]{2,1,0:T(1,128)}), f32[32,1,128]{2,1,0:T(1,128)S(1)}, u32[]{:S(2)}, u32[]{:S(2)}) %all-to-all-start.1) | async-done | bytes 16416 | tf_op jit(solution)/shard_map/all_to_all | solution.py:71
  191.3 0.5 broadcast.223
  191.8 0.7 reduce.8
  192.5 0.1 reshape.156
  192.6 0.1 fusion.8
  192.7 0.1 subtract_dynamic-update-slice_fusion.1
  192.8 0.1 subtract_dynamic-update-slice_fusion
  192.9 10.1 %all-reduce.2 = (f32[128]{0:T(128)S(1)}, f32[128]{0:T(128)S(1)}) all-reduce(f32[128]{0:T(128)S(1)} %subtract_dynamic-update-slice_fusion.1, f32[128]{0:T(128)S(1)} %subtract_dynamic-update-slice_fusion), channel_id=1, replica_groups=mesh['x'=4,'y'=4,'z'=16,'c'=2] {'x'}, use_global_device_ids=true, to_apply=%add | all-reduce | flops 256 | bytes 2048
  203.0 0.5 broadcast_select_fusion
  203.5 0.5 broadcast_select_fusion.1
  (11 shorter events, 0.1 us)
Async XLA Ops:
  7.2 173.0 %copy-start = (s32[65]{0:T(128)S(1)}, s32[65]{0:T(128)}, u32[]{:S(2)}) copy-start(s32[65]{0:T(128)} %param.9) | copy-start | bytes 784
  7.2 15.2 %all-to-all-start = ((bf16[4,32,256]{2,1,0:T(8,128)(2,1)}), bf16[4,32,256]{2,1,0:T(8,128)(2,1)S(1)}, u32[]{:S(2)}, u32[]{:S(2)}) async-start(bf16[4,32,256]{2,1,0:T(8,128)(2,1)} %bitcast.53), calls=%async_computation | async-start | bytes 131072 | tf_op jit(solution)/shard_map/all_to_all | solution.py:37
  11.5 85.6 %all-gather.7.cloned.1.call-start = ((), (), s32[]{:S(2)}) async-start(), calls=%async_computation.2 | async-start | bytes 2162688 | tf_op jit(solution)/shard_map/all_gather | solution.py:44
  23.2 134.1 %all-gather.9.cloned.1.call-start = ((), (), s32[]{:S(2)}) async-start(), calls=%async_computation.3 | async-start | bytes 2228224 | tf_op jit(solution)/shard_map/all_gather | solution.py:47
  167.3 24.0 %all-to-all-start.1 = ((f32[32,1,128]{2,1,0:T(1,128)}), f32[32,1,128]{2,1,0:T(1,128)S(1)}, u32[]{:S(2)}, u32[]{:S(2)}) async-start(f32[32,1,128]{2,1,0:T(1,128)} %reshape.155), calls=%async_computation.1 | async-start | bytes 32768 | tf_op jit(solution)/shard_map/all_to_all | solution.py:71
Sparse Core Ops, SparseCore 0:
  23.4 73.6 all-gather.6
  100.1 57.2 all-gather.8
where the time goes:
time: 211 us
  waiting for transfers between devices  105 us (50%)
  blocking collectives  54.3 us (26%)
  starting transfers between devices  17.2 us (8%)
  between operations  14.8 us (7%)
  local copies, waits for them, and re-layouts  7.86 us (4%)
  other arithmetic  6.01 us (3%)
  matrix products  5.9 us (3%)
    all_gather x1, waiting for transfers between devices, per_device(): weight = lax.all_gather(head_weight, ('x', 'y'), axis=0)  57.4 us
    all_gather x1, waiting for transfers between devices, per_device(): group_rows = lax.all_gather(normed, TOKEN_AXES, axis=0, tiled=True)  36.7 us
    all_gather x1, blocking collectives, per_device(): group_ids = lax.all_gather(target_ids, TOKEN_AXES, axis=0)  34.1 us
    all_to_all x1, starting transfers between devices, per_device(): lax.all_to_all(stats, TOKEN_AXES, split_axis=1, concat_axis=1, tiled=True)  12.8 us
    all_gather x1, blocking collectives, per_device(): gain_full = lax.all_gather(norm_gain, 'x', axis=0, tiled=True)  10.2 us
    unnamed x1, blocking collectives  10.1 us
    all_to_all x1, waiting for transfers between devices, per_device(): lax.all_to_all(stats, TOKEN_AXES, split_axis=1, concat_axis=1, tiled=True)  9.93 us
    dot_general x1, matrix products, per_device(): jnp.einsum('txd,xyde->tye', group_rows.reshape(-1, x_count, D // x_count)...  5.9 us
  transfers between devices with their start and end apart: 4, of which 3 were waited for; matrix products, arithmetic and copies ran while one was open for 3% of the time, Pallas kernels for 0%

commit v1 on v0

--- a/solution.py
+++ b/solution.py
@@ -3,6 +3,7 @@
 from jax import lax
 from jax.sharding import Mesh
 from jax.sharding import PartitionSpec as P
+from jax.lax import all_to_all, axis_size
 
 D = 1024
 SHORT = 128
@@ -35,7 +36,9 @@
     vocab_local = head_weight.shape[1]
     group_count = z_count * c_count
     rows = lax.all_to_all(hidden, "x", split_axis=0, concat_axis=1, tiled=True)
-    gain_full = lax.all_gather(norm_gain, "x", axis=0, tiled=True)
+    gain_full = jnp.concatenate(
+        all_to_all(jnp.stack([norm_gain for _ in range(axis_size("x"))]), "x", 0, 0), axis=0
+    )
     values = rows.astype(jnp.float32)
     squares = jnp.sum(values * values, axis=1, keepdims=True)
     normed = (

time: 211 us -> 217 us (1.028)
  waiting for transfers between devices: 105 us -> 111 us
    all_gather x1 -> x0, blocking collectives: 10.2 us -> none  [per_device(): gain_full = lax.all_gather(norm_gain, 'x', axis=0, tiled=True)]
    all_to_all x0 -> x1, blocking collectives: none -> 9.35 us  [per_device(): all_to_all(jnp.stack([norm_gain for _ in range(axis_size('x'))]), 'x', 0, 0)]
    all_to_all x1, waiting for transfers between devices: 0.01 us -> 5.51 us  [per_device(): rows = lax.all_to_all(hidden, 'x', split_axis=0, concat_axis=1, tiled=True)]
  transfers between devices with their start and end apart: 4 -> 4, of which waited for: 3 -> 4; matrix products, arithmetic and copies ran while one was open for 3% -> 3% of each run, Pallas kernels for 0% -> 0%
where the time goes in v1:
time: 217 us; the launch traced here: 216 us
  waiting for transfers between devices  111 us (51%)
  blocking collectives  53.5 us (25%)
  starting transfers between devices  16.2 us (7%)
  between operations  14.8 us (7%)
  local copies, waits for them, and re-layouts  8.41 us (4%)
  other arithmetic  6.68 us (3%)
  matrix products  5.9 us (3%)
    all_gather x1, waiting for transfers between devices, per_device(): weight = lax.all_gather(head_weight, ('x', 'y'), axis=0)  57.4 us
    all_gather x1, waiting for transfers between devices, per_device(): group_rows = lax.all_gather(normed, TOKEN_AXES, axis=0, tiled=True)  37.1 us
    all_gather x1, blocking collectives, per_device(): group_ids = lax.all_gather(target_ids, TOKEN_AXES, axis=0)  34.1 us
    all_to_all x1, starting transfers between devices, per_device(): lax.all_to_all(stats, TOKEN_AXES, split_axis=1, concat_axis=1, tiled=True)  12.8 us
    unnamed x1, blocking collectives  10.1 us
    all_to_all x1, waiting for transfers between devices, per_device(): lax.all_to_all(stats, TOKEN_AXES, split_axis=1, concat_axis=1, tiled=True)  9.93 us
    all_to_all x1, blocking collectives, per_device(): all_to_all(jnp.stack([norm_gain for _ in range(axis_size('x'))]), 'x', 0, 0)  9.35 us
    dot_general x1, matrix products, per_device(): jnp.einsum('txd,xyde->tye', group_rows.reshape(-1, x_count, D // x_count)...  5.9 us
  transfers between devices with their start and end apart: 4, of which 4 were waited for; matrix products, arithmetic and copies ran while one was open for 3% of the time, Pallas kernels for 0%

profile of v1, /device:TPU:32, one launch (start us, length us, event | category | flops | bytes accessed | tf_op | source)
XLA Modules:
  0.0 216.1 jit_solution(3382895561378717201)
XLA Ops:
  7.2 0.0 copy-start
  7.2 0.7 stack.22
  7.8 0.5 broadcast.226
  8.4 0.7 reduce.8
  9.0 9.3 %all_to_all.24 = bf16[4,2,128]{2,1,0:T(2,128)(2,1)S(1)} all-to-all(bf16[4,2,128]{2,1,0:T(2,128)(2,1)S(1)} %reshape.168), channel_id=1, replica_groups=mesh['x'=4,'y'=4,'z'=16,'c'=2] {'x'}, dimensions={0} | all-to-all | bytes 4096 | tf_op jit(solution)/shard_map/all_to_all | solution.py:40
  18.4 3.3 %all-to-all-start = ((bf16[4,32,256]{2,1,0:T(8,128)(2,1)}), bf16[4,32,256]{2,1,0:T(8,128)(2,1)S(1)}, u32[]{:S(2)}, u32[]{:S(2)}) async-start(bf16[4,32,256]{2,1,0:T(8,128)(2,1)} %bitcast.53), calls=%async_computation | async-start | bytes 131072 | tf_op jit(solution)/shard_map/all_to_all | solution.py:38
  21.7 0.0 all-gather.6.cloned.1.call-start
  21.8 5.5 %all-to-all-done = bf16[4,32,256]{2,1,0:T(8,128)(2,1)S(1)} async-done(((bf16[4,32,256]{2,1,0:T(8,128)(2,1)}), bf16[4,32,256]{2,1,0:T(8,128)(2,1)S(1)}, u32[]{:S(2)}, u32[]{:S(2)}) %all-to-all-start) | async-done | bytes 65568 | tf_op jit(solution)/shard_map/all_to_all | solution.py:38
  27.3 0.1 fusion.4
  27.4 0.7 multiply_convert_fusion
  28.1 0.0 all-gather.6.cloned.1.call-update
  28.2 0.0 all-gather.8.cloned.1.call-start
  28.2 0.7 all-gather.8.cloned.1.call-update
  28.9 34.1 %all-gather.2 = s32[32,1,128]{2,1,0:T(1,128)S(1)} all-gather(s32[1,1,128]{2,1,0:T(1,128)} %bitcast.55), channel_id=3, replica_groups=mesh['x'=4,'y'=4,'z'=16,'c'=2] {'z','c'}, dimensions={0}, use_global_device_ids=true | all-gather | bytes 16896 | tf_op jit(solution)/shard_map/all_gather | solution.py:48
  63.0 0.1 dynamic-slice_reduce_fusion
  63.1 0.1 eq.18
  63.2 1.3 dynamic-slice
  65.2 0.1 iota_add_fusion
  65.2 37.1 %all-gather.6.cloned.1.call-done = bf16[1024,1024]{1,0:T(8,128)(2,1)} async-done(((bf16[32,1024]{1,0:T(8,128)(2,1)}), bf16[1024,1024]{1,0:T(8,128)(2,1)}) %all-gather.6.cloned.1.call-update) | async-done | bytes 2097168 | tf_op jit(solution)/shard_map/all_gather | solution.py:47
  102.3 2.9 %copy.12 = bf16[1024,1024]{0,1:T(8,128)(2,1)S(1)} copy(bf16[1024,1024]{1,0:T(8,128)(2,1)} %all-gather.6.cloned.1.call-done) | data formatting | bytes 4194304 | tf_op jit(solution)/shard_map/all_gather | solution.py:47
  105.2 57.4 %all-gather.8.cloned.1.call-done = bf16[4096,251]{1,0:T(8,128)(2,1)} async-done(((bf16[256,251]{1,0:T(8,128)(2,1)}), bf16[4096,251]{1,0:T(8,128)(2,1)}) %all-gather.8.cloned.1.call-update) | async-done | bytes 2056208 | tf_op jit(solution)/shard_map/all_gather | solution.py:50
  162.6 5.9 %bitcast_reduce_fusion = (f32[1024]{0:T(1024)S(1)}, f32[1024,4,251,1]{0,2,1,3:T(8,128)}) fusion(bf16[1024,4,256,1]{0,2,3,1:T(8,128)(2,1)S(1)} %bitcast.46, bf16[4,4,256,251]{3,2,1,0:T(8,128)(2,1)} %bitcast.56), kind=kOutput, calls=%fused_computation.4 | convolution fusion | flops 2106567680 | bytes 8269824 | tf_op jit(solution)/shard_map/txd,xyde->tye/dot_general | solution.py:52
  168.5 0.1 stack.23
  168.5 2.9 %fusion.1 = (f32[1024]{0:T(1024)S(1)}, f32[1024]{0:T(1024)S(1)}, f32[1024]{0:T(1024)S(1)}) fusion(f32[1024,4,251,1]{0,2,1,3:T(8,128)} %get-tuple-element.16, f32[1024]{0:T(1024)S(1)} %get-tuple-element.15, s32[1024]{0:T(1024)S(1)} %eq.18, s32[4,251]{1,0:T(4,128)S(1)} %iota_add_fusion), kind=kLoop, calls=%fused_computation.6 | loop fusion | flops 7193600 | bytes 4136880 | tf_op jit(solution)/shard_map/reduce_sum | solution.py:66
  171.5 0.1 stack.26
  171.6 0.1 stack.25
  171.7 0.1 stack.24
  171.7 0.1 fusion.9
  171.8 0.7 reshape.170
  172.5 12.8 %all-to-all-start.2 = ((f32[32,1,128]{2,1,0:T(1,128)}), f32[32,1,128]{2,1,0:T(1,128)S(1)}, u32[]{:S(2)}, u32[]{:S(2)}) async-start(f32[32,1,128]{2,1,0:T(1,128)} %reshape.170), calls=%async_computation.2 | async-start | bytes 32768 | tf_op jit(solution)/shard_map/all_to_all | solution.py:74
  185.4 0.0 copy-done
  185.4 1.2 gather_fusion
  186.6 9.9 %all-to-all-done.2 = f32[32,1,128]{2,1,0:T(1,128)S(1)} async-done(((f32[32,1,128]{2,1,0:T(1,128)}), f32[32,1,128]{2,1,0:T(1,128)S(1)}, u32[]{:S(2)}, u32[]{:S(2)}) %all-to-all-start.2) | async-done | bytes 16416 | tf_op jit(solution)/shard_map/all_to_all | solution.py:74
  196.5 0.5 broadcast.227
  197.0 0.7 reduce.9
  197.7 0.1 reshape.171
  197.8 0.1 fusion.8
  198.0 0.1 subtract_dynamic-update-slice_fusion.1
  198.1 0.1 subtract_dynamic-update-slice_fusion
  198.2 10.1 %all-reduce.2 = (f32[128]{0:T(128)S(1)}, f32[128]{0:T(128)S(1)}) all-reduce(f32[128]{0:T(128)S(1)} %subtract_dynamic-update-slice_fusion.1, f32[128]{0:T(128)S(1)} %subtract_dynamic-update-slice_fusion), channel_id=1, replica_groups=mesh['x'=4,'y'=4,'z'=16,'c'=2] {'x'}, use_global_device_ids=true, to_apply=%add | all-reduce | flops 256 | bytes 2048
  208.2 0.5 broadcast_select_fusion
  208.8 0.5 broadcast_select_fusion.1
  (13 shorter events, 0.1 us)
Async XLA Ops:
  7.2 178.2 %copy-start = (s32[65]{0:T(128)S(1)}, s32[65]{0:T(128)}, u32[]{:S(2)}) copy-start(s32[65]{0:T(128)} %param.9) | copy-start | bytes 784
  18.4 8.9 %all-to-all-start = ((bf16[4,32,256]{2,1,0:T(8,128)(2,1)}), bf16[4,32,256]{2,1,0:T(8,128)(2,1)S(1)}, u32[]{:S(2)}, u32[]{:S(2)}) async-start(bf16[4,32,256]{2,1,0:T(8,128)(2,1)} %bitcast.53), calls=%async_computation | async-start | bytes 131072 | tf_op jit(solution)/shard_map/all_to_all | solution.py:38
  21.7 80.6 %all-gather.6.cloned.1.call-start = ((), (), s32[]{:S(2)}) async-start(), calls=%async_computation.3 | async-start | bytes 2162688 | tf_op jit(solution)/shard_map/all_gather | solution.py:47
  28.2 134.4 %all-gather.8.cloned.1.call-start = ((), (), s32[]{:S(2)}) async-start(), calls=%async_computation.4 | async-start | bytes 2228224 | tf_op jit(solution)/shard_map/all_gather | solution.py:50
  172.5 24.0 %all-to-all-start.2 = ((f32[32,1,128]{2,1,0:T(1,128)}), f32[32,1,128]{2,1,0:T(1,128)S(1)}, u32[]{:S(2)}, u32[]{:S(2)}) async-start(f32[32,1,128]{2,1,0:T(1,128)} %reshape.170), calls=%async_computation.2 | async-start | bytes 32768 | tf_op jit(solution)/shard_map/all_to_all | solution.py:74
Sparse Core Ops, SparseCore 0:
  28.3 73.9 all-gather.5
  105.3 57.1 all-gather.7
